TPU v7x, 128 devices: a whole 4x4x4 slice. The times are simulated.
128 devices in a mesh: row: 16 (over y, z), col: 8 (over x, core).
Axes of the slice: x: 4, y: 4, z: 4, core: 2. Of those that a mesh axis runs over, the one named last changes fastest.
Arguments:
- front: float32 [2, 8192, 4, 4096], P(None, 'row', None, 'col')
- child_blocks: float32 [2, 8192, 8192], P(None, 'row', 'col')
- index_maps: int32 [2, 8192], replicated, may hold values from 0 to 16383, as said below
Outputs:
- schur: float32 [2, 8192, 4, 4096], P(None, 'row', None, 'col')
- factor: float32 [2, 8192, 1024], P(None, 'row')
Inputs may be any that keep to these rules, and one draw needn't show every extreme that they name: Within one child the map names distinct front indices. Entry index_maps[h, (s * R + k) * 32 + i], with R the number of row indices, names an index in a block b of 512 indices with b mod R equal to k.
All inputs are finite; a program needn't handle non-finite values.
Results may differ from a plain program's by a relative error of at most 0.0001.
Values sent between devices are 32-bit elements; how exact they have to be, the bound alone decides.
A program may use at most 128 MiB of HBM per device.

v0:
```python
import jax
import jax.numpy as jnp
from jax import lax
from jax.sharding import PartitionSpec as P

NB = 512


def spread(value, axis, source):
    kept = jnp.where(lax.axis_index(axis) == source, value, 0).astype(value.dtype)
    return lax.psum(kept, axis)


def share_panel(values, root):
    return spread(values, "col", root)


def factor_panel(panel, section, my_row, row_count):
    pivot = spread(panel[:NB], "row", section)
    lower = jnp.linalg.cholesky(pivot)
    solved = lax.linalg.triangular_solve(
        lower, panel, left_side=False, lower=True, transpose_a=True
    )
    rows_local = panel.shape[0]
    block_ids = jnp.arange(rows_local, dtype=jnp.int32) // NB * row_count + my_row
    tiled = jnp.tile(lower, (rows_local // NB, 1))
    zeros = jnp.zeros_like(solved)
    picked = jnp.where((block_ids == section)[:, None], tiled, solved)
    return jnp.where((block_ids < section)[:, None], zeros, picked)


def column_rows(factor_rows, my_col, row_count, col_count):
    pieces = [
        spread(factor_rows, "row", my_col + turn * col_count)
        for turn in range(row_count // col_count)
    ]
    blocks = factor_rows.shape[0] // NB
    shaped = [piece.reshape(blocks, NB, NB) for piece in pieces]
    return jnp.stack(shaped, axis=1).reshape(-1, NB)


def outer_update(matrix, left_rows, right_rows):
    return matrix - jnp.dot(
        left_rows, right_rows.T, precision=lax.Precision.HIGHEST, preferred_element_type=jnp.float32
    )


def group_columns(blocks, row_count, col_count):
    children, height, width = blocks.shape
    ratio = row_count // col_count
    shaped = blocks.reshape(children, height, ratio, ratio, col_count, -1)
    return shaped.transpose(0, 1, 4, 2, 3, 5).reshape(children, height, width)


def local_position(global_ids, count):
    return global_ids // (NB * count) * NB + global_ids % NB


def inverse_map(positions, length):
    arriving = jnp.arange(positions.shape[0], dtype=jnp.int32)
    inverse = jnp.full((length,), -1, jnp.int32).at[positions].set(arriving)
    return (jnp.maximum(inverse, 0), inverse >= 0)


def on_device(front, child_blocks, index_maps):
    row_blocks, block_rows, col_blocks, block_cols = front.shape
    rows_local = row_blocks * block_rows
    cols_local = col_blocks * block_cols
    row_count = lax.axis_size("row")
    col_count = lax.axis_size("col")
    my_row = lax.axis_index("row")
    my_col = lax.axis_index("col")
    summed = front.reshape(rows_local, cols_local)
    outgoing = group_columns(child_blocks, row_count, col_count)
    arrived = lax.all_to_all(
        lax.all_to_all(outgoing, "row", split_axis=1, concat_axis=1, tiled=True),
        "col",
        split_axis=2,
        concat_axis=2,
        tiled=True,
    )
    children = child_blocks.shape[0]
    ratio = row_count // col_count
    row_ids = lax.dynamic_index_in_dim(
        index_maps.reshape(children, row_count, row_count, -1), my_row, 2, keepdims=False
    ).reshape(children, -1)
    col_ids = lax.dynamic_index_in_dim(
        index_maps.reshape(children, col_count, ratio, ratio, col_count, -1),
        my_col,
        4,
        keepdims=False,
    ).reshape(children, -1)
    local_rows = local_position(row_ids, row_count)
    local_cols = local_position(col_ids, col_count)
    for child in range(children):
        row_take, row_valid = inverse_map(local_rows[child], rows_local)
        col_take, col_valid = inverse_map(local_cols[child], cols_local)
        widened = jnp.where(col_valid[None, :], jnp.take(arrived[child], col_take, axis=1), 0.0)
        placed = jnp.where(row_valid[:, None], jnp.take(widened, row_take, axis=0), 0.0)
        summed = summed + placed
    panel = share_panel(summed[:, :NB], 0)
    outputs = []
    for section in range(2):
        factor_rows = factor_panel(panel, section, my_row, row_count)
        factor_cols = column_rows(factor_rows, my_col, row_count, col_count)
        summed = outer_update(summed, factor_rows, factor_cols)
        outputs.append(factor_rows)
        if section == 0:
            panel = share_panel(summed[:, :NB], 1)
    schur = summed.reshape(front.shape)
    factor = jnp.concatenate(outputs, axis=1).reshape(row_blocks, block_rows, 2 * NB)
    return (schur, factor)


def solution(mesh):
    placed = (P(None, "row", None, "col"), P(None, "row", "col"), P())
    return jax.shard_map(
        on_device,
        mesh=mesh,
        in_specs=placed,
        out_specs=(P(None, "row", None, "col"), P(None, "row", None)),
        check_vma=False,
    )
```

profile of v0, /device:TPU:1, one launch (start us, length us, event | category | flops | bytes accessed | tf_op | source)
XLA Modules:
  0.0 1176.0 jit_solution(15224041002027477895)
XLA Ops:
  24.8 57.9 %all_to_all.10 = f32[2,512,1024]{2,0,1:T(2,128)} all-to-all(f32[2,512,1024]{2,0,1:T(2,128)} %copy.68), channel_id=1, replica_groups=mesh['row'=16,'col'=8] {'row'}, dimensions={1} | all-to-all | bytes 8388608 | tf_op jit(solution)/shard_map/all_to_all | solution.py:76
  99.7 10.9 copy.110
  134.1 13.8 %all-to-all-done.1 = f32[2,512,1024]{1,0,2:T(2,128)} async-done(((f32[2,512,1024]{1,0,2:T(2,128)}), f32[2,512,1024]{1,0,2:T(2,128)}, u32[]{:S(2)}, u32[]{:S(2)}) %all-to-all-start.1) | async-done | bytes 4194336 | tf_op jit(solution)/shard_map/all_to_all | solution.py:75
  156.7 11.1 gather_fusion
  177.2 11.0 gather_fusion.1
  215.7 11.0 gather_fusion.3
  236.0 9.9 fusion
  250.9 60.6 %all-reduce.10.cloned.1.call-done = f32[1024,512]{0,1:T(8,128)} async-done(((f32[1024,512]{0,1:T(8,128)}), f32[1024,512]{0,1:T(8,128)}) %all-reduce.10.cloned.1.call-update) | async-done | bytes 2097168 | tf_op jit(solution)/shard_map/psum | solution.py:11
  314.1 88.5 %all-reduce.12.cloned.1.call-done = f32[512,512]{0,1:T(8,128)} async-done(((f32[512,512]{0,1:T(8,128)}), f32[512,512]{0,1:T(8,128)}) %all-reduce.12.cloned.1.call-update) | async-done | bytes 1048592 | tf_op jit(solution)/shard_map/psum | solution.py:11
  404.5 11.7 cholesky.286
  416.4 9.8 custom-call.27
  426.9 11.7 cholesky.305
  439.9 10.0 custom-call.28
  450.6 11.7 cholesky.326
  473.4 11.7 cholesky.343
  490.3 11.9 %while.4 = (s32[]{:T(128)}, f32[512,512]{1,0:T(8,128)}, s32[4,2]{0,1:T(2,128)S(1)}, f32[4,128,128]{2,1,0:T(8,128)S(1)}, s32[]{:T(128)}) while((s32[]{:T(128)}, f32[512,512]{1,0:T(8,128)}, s32[4,2]{0,1:T(2,128)S(1)}, f32[4,128,128]{2,1,0:T(8,128)S(1)}, s32[]{:T(128)}) %tuple.76), condition=%wide.while_cond, body=%wide.while_body.sunk | while | flops 2 | bytes 131181 | solution.py:21
  502.2 39.3 %custom-call.30 = f32[4,128,128]{1,2,0:T(8,128)S(1)} custom-call(f32[4,128,128]{2,1,0:T(8,128)S(1)} %get-tuple-element.20), custom_call_target="InvertDiagBlocksLowerTriangular" | custom-call | tf_op jit(solution)/shard_map/triangular_solve/custom-call.3 | solution.py:21
  564.4 104.1 %all-reduce.20.cloned.1.call-done = (f32[2,1,512,512]{3,2,1,0:T(8,128)}, f32[2,1,512,512]{3,2,1,0:T(8,128)}) async-done(((f32[2,1,512,512]{3,2,1,0:T(8,128)}, f32[2,1,512,512]{3,2,1,0:T(8,128)}), (f32[2,1,512,512]{3,2,1,0:T(8,128)}, f32[2,1,512,512]{3,2,1,0:T(8,128)})) %all-reduce.20.cloned.1.call-update) | async-done | bytes 4194320 | tf_op jit(solution)/shard_map/psum | solution.py:11
  671.2 17.1 %convolution_subtract_fusion.1 = f32[1024,2048]{0,1:T(8,128)S(1)} fusion(f32[1024,2048]{0,1:T(8,128)} %copy-done.1, f32[1024,512]{0,1:T(8,128)S(1)} %get-tuple-element.55, f32[2048,512]{1,0:T(8,128)S(1)} %bitcast.156), kind=kOutput, calls=%fused_computation.22 | convolution fusion | flops 12886999040 | bytes 23068672 | tf_op jit(solution)/shard_map/dot_general | solution.py:43
  693.3 63.7 %all-reduce.14.cloned.1.call-done = f32[1024,512]{0,1:T(8,128)} async-done(((f32[1024,512]{0,1:T(8,128)}), f32[1024,512]{0,1:T(8,128)}) %all-reduce.14.cloned.1.call-update) | async-done | bytes 2097168 | tf_op jit(solution)/shard_map/psum | solution.py:11
  759.6 88.4 %all-reduce.16.cloned.1.call-done = f32[512,512]{0,1:T(8,128)} async-done(((f32[512,512]{0,1:T(8,128)}), f32[512,512]{0,1:T(8,128)}) %all-reduce.16.cloned.1.call-update) | async-done | bytes 1048592 | tf_op jit(solution)/shard_map/psum | solution.py:11
  853.0 11.7 cholesky.358
  877.3 11.7 cholesky.377
  890.3 10.2 custom-call.32
  902.1 11.7 cholesky.398
  925.7 11.7 cholesky.415
  942.4 11.1 while.5
  953.5 39.3 %custom-call.34 = f32[4,128,128]{1,2,0:T(8,128)S(1)} custom-call(f32[4,128,128]{2,1,0:T(8,128)S(1)} %get-tuple-element.21), custom_call_target="InvertDiagBlocksLowerTriangular" | custom-call | tf_op jit(solution)/shard_map/triangular_solve/custom-call.3 | solution.py:21
  1028.6 94.9 %all-reduce.18.cloned.1.call-done = (f32[2,1,512,512]{3,2,1,0:T(8,128)}, f32[2,1,512,512]{3,2,1,0:T(8,128)}) async-done(((f32[2,1,512,512]{3,2,1,0:T(8,128)}, f32[2,1,512,512]{3,2,1,0:T(8,128)}), (f32[2,1,512,512]{3,2,1,0:T(8,128)}, f32[2,1,512,512]{3,2,1,0:T(8,128)})) %all-reduce.18.cloned.1.call-update) | async-done | bytes 4194320 | tf_op jit(solution)/shard_map/psum | solution.py:11
  1126.4 17.7 %convolution_subtract_fusion = f32[1024,2048]{0,1:T(8,128)} fusion(f32[1024,2048]{0,1:T(8,128)} %copy-done, f32[1024,512]{0,1:T(8,128)S(1)} %copy-done.3, f32[2048,512]{1,0:T(8,128)S(1)} %bitcast.155), kind=kOutput, calls=%fused_computation.21 | convolution fusion | flops 12886999040 | bytes 23068672 | tf_op jit(solution)/shard_map/dot_general | solution.py:43
  1144.1 11.7 reshape.242
  1155.8 13.2 %copy.92 = f32[2,512,4,512]{3,2,1,0:T(4,128)} copy(f32[2,512,4,512]{1,0,3,2:T(2,128)} %reshape.242) | data formatting | bytes 16777216
  (195 shorter events, 267.9 us)
Async XLA Ops:
  91.9 7.1 copy-start.15
  91.9 56.0 %all-to-all-start.1 = ((f32[2,512,1024]{1,0,2:T(2,128)}), f32[2,512,1024]{1,0,2:T(2,128)}, u32[]{:S(2)}, u32[]{:S(2)}) async-start(f32[2,512,1024]{1,0,2:T(2,128)} %copy.69), calls=%async_computation.1 | async-start | bytes 8388608 | tf_op jit(solution)/shard_map/all_to_all | solution.py:75
  99.0 212.5 %all-reduce.10.cloned.1.call-start = ((), (), s32[]{:S(2)}) async-start(), calls=%async_computation.2 | async-start | bytes 4194304 | tf_op jit(solution)/shard_map/psum | solution.py:11
  245.9 3.4 copy-start.1
  250.8 151.8 %all-reduce.12.cloned.1.call-start = ((), (), s32[]{:S(2)}) async-start(), calls=%async_computation.3 | async-start | bytes 2097152 | tf_op jit(solution)/shard_map/psum | solution.py:11
  313.8 354.7 %all-reduce.20.cloned.1.call-start = ((), (), s32[]{:S(2)}) async-start(), calls=%async_computation.7 | async-start | bytes 8388608 | tf_op jit(solution)/shard_map/psum | solution.py:11
  402.6 1.7 copy-start.10
  502.2 43.3 %copy-start.4 = (f32[1024,512]{0,1:T(8,128)S(1)}, f32[1024,512]{0,1:T(8,128)}, u32[]{:S(2)}) copy-start(f32[1024,512]{0,1:T(8,128)} %all-reduce.10.cloned.1.call-done) | copy-start | bytes 6291460
  547.8 2.3 copy-start.8
  553.8 1.0 copy-start.9
  553.8 1.2 copy-start.14
  564.2 192.8 %all-reduce.14.cloned.1.call-start = ((), (), s32[]{:S(2)}) async-start(), calls=%async_computation.4 | async-start | bytes 4194304 | tf_op jit(solution)/shard_map/psum | solution.py:11
  688.3 3.4 copy-start
  693.2 154.7 %all-reduce.16.cloned.1.call-start = ((), (), s32[]{:S(2)}) async-start(), calls=%async_computation.5 | async-start | bytes 2097152 | tf_op jit(solution)/shard_map/psum | solution.py:11
  759.3 364.2 %all-reduce.18.cloned.1.call-start = ((), (), s32[]{:S(2)}) async-start(), calls=%async_computation.6 | async-start | bytes 8388608 | tf_op jit(solution)/shard_map/psum | solution.py:11
  848.0 2.6 copy-start.11
  852.1 1.0 copy-start.12
  992.8 4.2 copy-start.5
  999.2 2.3 copy-start.6
  1007.4 1.0 copy-start.7
  1007.4 1.2 copy-start.13
  1010.5 1.3 copy-start.2
  1123.5 2.9 copy-start.3
Sparse Core Ops, SparseCore 0:
  250.9 60.5 all-reduce.9
  315.3 87.2 all-reduce.11
  564.3 104.1 all-reduce.19
  693.4 63.6 all-reduce.13
  760.7 87.2 all-reduce.15
  1019.3 104.1 all-reduce.17
where the time goes:
time: 1190 us; the launch traced here: 1180 us
  waiting for transfers between devices  514 us (43%)
  other arithmetic  284 us (24%)
  local copies, waits for them, and re-layouts  229 us (19%)
  matrix products  62.1 us (5%)
  blocking collectives  57.9 us (5%)
  between operations  20.1 us (2%)
    psum x6, waiting for transfers between devices, spread(): return lax.psum(kept, axis)  500 us
    another operation x30, other arithmetic, factor_panel(): lower = jnp.linalg.cholesky(pivot)  159 us
    another operation x5, other arithmetic, factor_panel(): lax.linalg.triangular_solve(lower, panel, left_side=False, lower=True, tr...  82.4 us
    all_to_all x1, blocking collectives, on_device(): lax.all_to_all(outgoing, 'row', split_axis=1, concat_axis=1, tiled=True)  57.9 us
    unnamed x38, local copies, waits for them, and re-layouts  46.2 us
    gather x4, local copies, waits for them, and re-layouts, on_device(): jnp.take(widened, row_take, axis=0)  40.6 us
    dot_general x2, matrix products, outer_update(): jnp.dot(left_rows, right_rows.T, precision=lax.Precision.HIGHEST, preferr...  34.9 us
  transfers between devices with their start and end apart: 7, of which 7 were waited for; matrix products, arithmetic and copies ran while one was open for 4% of the time, Pallas kernels for 0%

commit v1 on v0

--- a/solution.py
+++ b/solution.py
@@ -8,7 +8,7 @@
 
 def spread(value, axis, source):
     kept = jnp.where(lax.axis_index(axis) == source, value, 0).astype(value.dtype)
-    return lax.psum(kept, axis)
+    return jnp.sum(lax.all_gather(kept, axis), axis=0)
 
 
 def share_panel(values, root):

time: 1190 us -> 2050 us (1.72)
  waiting for transfers between devices: 514 us -> 1080 us
  local copies, waits for them, and re-layouts: 229 us -> 447 us
  other arithmetic: 284 us -> 352 us
    all_gather x0 -> x8, waiting for transfers between devices: none -> 1070 us  [spread(): return jnp.sum(lax.all_gather(kept, axis), axis=0)]
    psum x6 -> x0, waiting for transfers between devices: 500 us -> none  [spread(): return lax.psum(kept, axis)]
    unnamed x38 -> x46, local copies, waits for them, and re-layouts: 46.2 us -> 266 us
    reduce_sum x0 -> x8, other arithmetic: none -> 66.4 us  [spread(): return jnp.sum(lax.all_gather(kept, axis), axis=0)]
  transfers between devices with their start and end apart: 7 -> 9, of which waited for: 7 -> 9; matrix products, arithmetic and copies ran while one was open for 4% -> 7% of each run, Pallas kernels for 0% -> 0%
where the time goes in v1:
time: 2050 us; the launch traced here: 2040 us
  waiting for transfers between devices  1080 us (53%)
  local copies, waits for them, and re-layouts  447 us (22%)
  other arithmetic  352 us (17%)
  matrix products  69 us (3%)
  blocking collectives  57.9 us (3%)
  between operations  21.2 us (1%)
    all_gather x8, waiting for transfers between devices, spread(): return jnp.sum(lax.all_gather(kept, axis), axis=0)  1070 us
    unnamed x46, local copies, waits for them, and re-layouts  266 us
    another operation x30, other arithmetic, factor_panel(): lower = jnp.linalg.cholesky(pivot)  159 us
    another operation x5, other arithmetic, factor_panel(): lax.linalg.triangular_solve(lower, panel, left_side=False, lower=True, tr...  83.9 us
    reduce_sum x8, other arithmetic, spread(): return jnp.sum(lax.all_gather(kept, axis), axis=0)  66.4 us
    all_to_all x1, blocking collectives, on_device(): lax.all_to_all(outgoing, 'row', split_axis=1, concat_axis=1, tiled=True)  57.9 us
  transfers between devices with their start and end apart: 9, of which 9 were waited for; matrix products, arithmetic and copies ran while one was open for 7% of the time, Pallas kernels for 0%

profile of v1, /device:TPU:1, one launch (start us, length us, event | category | flops | bytes accessed | tf_op | source)
XLA Modules:
  0.0 2038.7 jit_solution(17357912315326132284)
XLA Ops:
  24.8 57.9 %all_to_all.10 = f32[2,512,1024]{2,0,1:T(2,128)} all-to-all(f32[2,512,1024]{2,0,1:T(2,128)} %copy.64), channel_id=1, replica_groups=mesh['row'=16,'col'=8] {'row'}, dimensions={1} | all-to-all | bytes 8388608 | tf_op jit(solution)/shard_map/all_to_all | solution.py:76
  133.9 14.1 all-to-all-done.1
  251.3 81.9 %all-gather.17.cloned.1.call-done = f32[8192,512]{0,1:T(8,128)} async-done(((f32[1024,512]{0,1:T(8,128)}), f32[8192,512]{0,1:T(8,128)}) %all-gather.17.cloned.1.call-update) | async-done | bytes 16777232 | tf_op jit(solution)/shard_map/all_gather | solution.py:11
  333.1 19.7 copy.107
  364.4 106.7 %all-gather.19.cloned.1.call-done = f32[8192,512]{0,1:T(8,128)} async-done(((f32[512,512]{0,1:T(8,128)}), f32[8192,512]{0,1:T(8,128)}) %all-gather.19.cloned.1.call-update) | async-done | bytes 16777232 | tf_op jit(solution)/shard_map/all_gather | solution.py:11
  471.1 20.1 copy.108
  504.8 11.7 cholesky.286
  529.7 11.9 cholesky.305
  553.7 11.7 cholesky.326
  577.8 11.7 cholesky.343
  608.3 40.3 %custom-call.30 = f32[4,128,128]{1,2,0:T(8,128)S(1)} custom-call(f32[4,128,128]{2,1,0:T(8,128)} %copy-done.12), custom_call_target="InvertDiagBlocksLowerTriangular" | custom-call | tf_op jit(solution)/shard_map/triangular_solve/custom-call.3 | solution.py:21
  664.3 195.3 %all-gather.21.cloned.1.call-done = f32[16384,512]{0,1:T(8,128)} async-done(((f32[1024,512]{0,1:T(8,128)}), f32[16384,512]{0,1:T(8,128)}) %all-gather.21.cloned.1.call-update) | async-done | bytes 33554448 | tf_op jit(solution)/shard_map/all_gather | solution.py:11
  859.6 32.7 %copy.110 = f32[64,8,16,1024]{3,2,1,0:T(8,128)S(1)} copy(f32[64,8,16,1024]{3,1,2,0:T(8,128)} %bitcast.198) | data formatting | bytes 67108864
  905.0 153.6 %all-gather.23.cloned.1.call-done = f32[16384,512]{0,1:T(8,128)} async-done(((f32[1024,512]{0,1:T(8,128)}), f32[16384,512]{0,1:T(8,128)}) %all-gather.23.cloned.1.call-update) | async-done | bytes 33554448 | tf_op jit(solution)/shard_map/all_gather | solution.py:11
  1058.6 32.5 %copy.111 = f32[64,8,16,1024]{3,2,1,0:T(8,128)S(1)} copy(f32[64,8,16,1024]{3,1,2,0:T(8,128)} %bitcast.200) | data formatting | bytes 67108864
  1106.4 17.5 convolution_subtract_fusion.1
  1128.9 85.0 %all-gather.25.cloned.1.call-done = f32[8192,512]{0,1:T(8,128)} async-done(((f32[1024,512]{0,1:T(8,128)}), f32[8192,512]{0,1:T(8,128)}) %all-gather.25.cloned.1.call-update) | async-done | bytes 16777232 | tf_op jit(solution)/shard_map/all_gather | solution.py:11
  1214.0 19.8 copy.112
  1248.1 105.4 %all-gather.27.cloned.1.call-done = f32[8192,512]{0,1:T(8,128)} async-done(((f32[512,512]{0,1:T(8,128)}), f32[8192,512]{0,1:T(8,128)}) %all-gather.27.cloned.1.call-update) | async-done | bytes 16777232 | tf_op jit(solution)/shard_map/all_gather | solution.py:11
  1353.4 20.2 copy.113
  1387.2 11.7 cholesky.358
  1412.1 12.1 cholesky.377
  1436.3 11.7 cholesky.398
  1460.1 11.7 cholesky.415
  1490.9 40.3 %custom-call.34 = f32[4,128,128]{1,2,0:T(8,128)S(1)} custom-call(f32[4,128,128]{2,1,0:T(8,128)} %copy-done.11), custom_call_target="InvertDiagBlocksLowerTriangular" | custom-call | tf_op jit(solution)/shard_map/triangular_solve/custom-call.3 | solution.py:21
  1558.5 185.5 %all-gather.29.cloned.1.call-done = f32[16384,512]{0,1:T(8,128)} async-done(((f32[1024,512]{0,1:T(8,128)}), f32[16384,512]{0,1:T(8,128)}) %all-gather.29.cloned.1.call-update) | async-done | bytes 33554448 | tf_op jit(solution)/shard_map/all_gather | solution.py:11
  1744.0 32.5 %copy.115 = f32[64,8,16,1024]{3,2,1,0:T(8,128)S(1)} copy(f32[64,8,16,1024]{3,1,2,0:T(8,128)} %bitcast.199) | data formatting | bytes 67108864
  1786.7 156.3 %all-gather.31.cloned.1.call-done = f32[16384,512]{0,1:T(8,128)} async-done(((f32[1024,512]{0,1:T(8,128)}), f32[16384,512]{0,1:T(8,128)}) %all-gather.31.cloned.1.call-update) | async-done | bytes 33554448 | tf_op jit(solution)/shard_map/all_gather | solution.py:11
  1943.0 32.5 %copy.116 = f32[64,8,16,1024]{3,2,1,0:T(8,128)S(1)} copy(f32[64,8,16,1024]{3,1,2,0:T(8,128)} %bitcast.201) | data formatting | bytes 67108864
  1989.0 17.5 convolution_subtract_fusion
  2006.5 11.7 reshape.242
  2018.2 13.2 copy.88
  (219 shorter events, 454.1 us)
Async XLA Ops:
  91.9 7.1 copy-start.10
  91.9 56.0 %all-to-all-start.1 = ((f32[2,512,1024]{1,0,2:T(2,128)}), f32[2,512,1024]{1,0,2:T(2,128)}, u32[]{:S(2)}, u32[]{:S(2)}) async-start(f32[2,512,1024]{1,0,2:T(2,128)} %copy.65), calls=%async_computation.1 | async-start | bytes 8388608 | tf_op jit(solution)/shard_map/all_to_all | solution.py:75
  99.0 234.1 %all-gather.17.cloned.1.call-start = ((), (), s32[]{:S(2)}) async-start(), calls=%async_computation.2 | async-start | bytes 18874368 | tf_op jit(solution)/shard_map/all_gather | solution.py:11
  245.9 3.4 copy-start.1
  250.8 220.3 %all-gather.19.cloned.1.call-start = ((), (), s32[]{:S(2)}) async-start(), calls=%async_computation.3 | async-start | bytes 17825792 | tf_op jit(solution)/shard_map/all_gather | solution.py:11
  359.3 500.4 %all-gather.21.cloned.1.call-start = ((), (), s32[]{:S(2)}) async-start(), calls=%async_computation.4 | async-start | bytes 35651584 | tf_op jit(solution)/shard_map/all_gather | solution.py:11
  503.8 1.0 copy-start.4
  607.6 0.7 copy-start.12
  648.6 3.4 copy-start.7
  648.6 6.7 copy-start.9
  662.7 395.9 %all-gather.23.cloned.1.call-start = ((), (), s32[]{:S(2)}) async-start(), calls=%async_computation.5 | async-start | bytes 35651584 | tf_op jit(solution)/shard_map/all_gather | solution.py:11
  664.3 549.7 %all-gather.25.cloned.1.call-start = ((), (), s32[]{:S(2)}) async-start(), calls=%async_computation.6 | async-start | bytes 18874368 | tf_op jit(solution)/shard_map/all_gather | solution.py:11
  1124.0 3.4 copy-start
  1128.9 224.6 %all-gather.27.cloned.1.call-start = ((), (), s32[]{:S(2)}) async-start(), calls=%async_computation.7 | async-start | bytes 17825792 | tf_op jit(solution)/shard_map/all_gather | solution.py:11
  1239.2 1.3 copy-start.3
  1241.6 502.4 %all-gather.29.cloned.1.call-start = ((), (), s32[]{:S(2)}) async-start(), calls=%async_computation.8 | async-start | bytes 35651584 | tf_op jit(solution)/shard_map/all_gather | solution.py:11
  1386.2 1.0 copy-start.5
  1490.1 0.7 copy-start.11
  1531.2 4.5 copy-start.6
  1531.2 7.9 copy-start.8
  1547.0 396.0 %all-gather.31.cloned.1.call-start = ((), (), s32[]{:S(2)}) async-start(), calls=%async_computation.9 | async-start | bytes 35651584 | tf_op jit(solution)/shard_map/all_gather | solution.py:11
  1986.1 2.9 copy-start.2
Sparse Core Ops, SparseCore 0:
  250.9 82.1 all-gather.16
  359.4 111.6 all-gather.18
  662.8 196.7 all-gather.20
  861.7 196.8 all-gather.22
  1129.0 84.9 all-gather.24
  1241.8 111.6 all-gather.26
  1547.1 196.8 all-gather.28
  1746.2 196.8 all-gather.30
